TPU v7x, 32 devices: a whole 2x2x4 slice. The times are simulated.
32 devices in a mesh: spot: 4 (over x, core), cell: 8 (over z, y).
Axes of the slice: x: 2, y: 2, z: 4, core: 2. Of those that a mesh axis runs over, the one named last changes fastest.
Arguments:
- logits: float32 [4096, 4096], P('cell', 'spot'), may hold values from -6 to 6
- expression: float32 [4096, 2048], P('cell', 'spot'), may hold values from 0.05 to 5
- spatial: float32 [2048, 4096], P('cell', 'spot'), may hold values from 0.05 to 5
- density: float32 [4096], P('spot'), may hold values from 0.2 to 5
- slide_ids: int32 [4096], replicated, may hold values from 0 to 2, as said below
- spot_valid: int32 [4096], replicated, may hold values 0 or 1
- neighbours: int32 [4096, 6], P('spot'), may hold values from -1 to 4095, as said below
Outputs:
- gene_loss: float32 [], replicated
- spot_loss: float32 [], replicated
- density_loss: float32 [], replicated
- grad_logits: float32 [4096, 4096], P('cell', 'spot')
- grad_expr: float32 [4096, 2048], P('cell', 'spot')
- rms_weights: float32 [], replicated
- rms_pred: float32 [], replicated
- rms_smooth: float32 [], replicated
Inputs may be any that keep to these rules, and one draw needn't show every extreme that they name: `slide_ids`: slide ids never fall along the spots, and each of the 3 slides holds whole grid rows of 64 spots. `neighbours`: spots lie row by row on a hexagonal grid with 64 spots a row, odd rows shifted; every listed neighbour is an adjacent grid spot, at most 65 away in index.
All inputs are finite; a program needn't handle non-finite values.
Results may differ from a plain program's by a relative error of at most 0.0003.
Values sent between devices are 32-bit elements; how exact they have to be, the bound alone decides.
No kernel may reach another device: no remote copies, remote signals or barrier semaphores. Data moves between devices by JAX's collectives and lax.ppermute only.
A program may use at most 128 MiB of HBM per device.

v0:
```python
import jax
import jax.numpy as jnp
from jax import lax
from jax.sharding import PartitionSpec as P

GENES = 2048
ROW = 64
SLIDES = 3
epsilon = 1e-06
highest = lax.Precision.HIGHEST


def padded_2(shard, sides, width):
    for axis, dim in sides:
        peers, length = (lax.axis_size(axis), shard.shape[dim])
        up = [(i, (i + 1) % peers) for i in range(peers - 1)]
        down = [(j, i) for i, j in up]
        last = lax.slice_in_dim(shard, length - width, length, axis=dim)
        first = lax.slice_in_dim(shard, 0, width, axis=dim)
        before = lax.ppermute(last, axis, up)
        after = lax.ppermute(first, axis, down)
        shard = jnp.concatenate([before, shard, after], axis=dim)
    return shard


def passed_along(block, axis, distance):
    devices = range(lax.axis_size(axis))
    route = [(i - distance, i) for i in devices if i - distance in devices]
    return lax.ppermute(block, axis, route)


def shards(logits, expression, spatial, density, slide_ids, spot_valid, neighbours):
    local_cells, local_spots = logits.shape
    local_genes = spatial.shape[0]
    total_cells = local_cells * lax.axis_size("cell")
    total_spots = local_spots * lax.axis_size("spot")
    margin = ROW + 1
    offset = lax.axis_index("spot") * local_spots
    valid_all = spot_valid.astype(jnp.float32)
    nvalid = jnp.sum(valid_all)
    valid_here = lax.dynamic_slice_in_dim(valid_all, offset, local_spots)
    slide_here = lax.dynamic_slice_in_dim(slide_ids, offset, local_spots)
    clamped = jnp.maximum(neighbours, 0)
    linked = (
        (neighbours >= 0) & (spot_valid[clamped] == 1) & (slide_ids[clamped] == slide_here[:, None])
    ).astype(jnp.float32)
    counts = 1.0 + jnp.sum(linked, axis=1)
    position = jnp.clip(clamped - offset + margin, 0, local_spots + 2 * margin - 1)
    members = (slide_here[:, None] == jnp.arange(SLIDES, dtype=jnp.int32)[None, :]).astype(
        jnp.float32
    )
    local_max = jnp.max(logits, axis=0)
    column_max = lax.pmax(local_max, "cell")
    raised = jnp.exp(logits - column_max)
    column_sum = lax.psum(jnp.sum(raised, axis=0), "cell")
    mapping = raised / column_sum
    genes_all = lax.all_gather(expression, "spot", axis=1, tiled=True)
    columns = genes_all
    predicted = lax.psum_scatter(
        lax.dot_general(columns, mapping, (((0,), (0,)), ((), ())), precision=highest),
        "cell",
        scatter_dimension=0,
        tiled=True,
    )
    padded = padded_2(predicted, (("spot", 1),), margin)
    summed = predicted
    for k in range(6):
        summed = summed + linked[:, k][None, :] * jnp.take(padded, position[:, k], axis=1)
    smoothed = summed / counts[None, :]
    spot_inner, spot_own, spot_target, row_sums = lax.psum(
        (
            jnp.sum(smoothed * spatial, axis=0),
            jnp.sum(smoothed * smoothed, axis=0),
            jnp.sum(spatial * spatial, axis=0),
            jnp.sum(predicted, axis=0),
        ),
        "cell",
    )
    weighted = valid_here[None, :]
    gene_inner, gene_own, gene_target, row_tot, target_tot = lax.psum(
        (
            jnp.sum(weighted * smoothed * spatial, axis=1),
            jnp.sum(weighted * smoothed * smoothed, axis=1),
            jnp.sum(weighted * spatial * spatial, axis=1),
            jnp.sum(members * (valid_here * row_sums)[:, None], axis=0),
            jnp.sum(members * (valid_here * density)[:, None], axis=0),
        ),
        "spot",
    )
    gene_scale = lax.rsqrt((gene_own + epsilon) * (gene_target + epsilon))
    cos_gene = gene_inner * gene_scale
    spot_scale = lax.rsqrt((spot_own + epsilon) * (spot_target + epsilon))
    cos_spot = spot_inner * spot_scale
    target = density / jnp.sum(members * target_tot[None, :], axis=1)
    slide_rows = jnp.sum(members * row_tot[None, :], axis=1)
    predicted_share = row_sums / slide_rows
    kl_terms = valid_here * target * (jnp.log(target) - jnp.log(predicted_share))
    grad_smooth = (
        -total_cells
        * weighted
        * (spatial - (gene_inner / (gene_own + epsilon))[:, None] * smoothed)
        * gene_scale[:, None]
    )
    grad_smooth = (
        grad_smooth
        - total_cells
        * total_spots
        / nvalid
        * weighted
        * (spatial - (spot_inner / (spot_own + epsilon))[None, :] * smoothed)
        * spot_scale[None, :]
    )
    spread_in = grad_smooth / counts[None, :]
    spread = jnp.zeros((local_genes, local_spots + 2 * margin), jnp.float32)
    for k in range(6):
        spread = spread.at[:, position[:, k]].add(linked[:, k][None, :] * spread_in)
    grad_pred = spread_in + spread[:, margin : margin + local_spots]
    from_next = passed_along(spread[:, :margin], "spot", -1)
    from_prev = passed_along(spread[:, margin + local_spots :], "spot", 1)
    grad_pred = grad_pred.at[:, local_spots - margin :].add(from_next)
    grad_pred = grad_pred.at[:, :margin].add(from_prev)
    grad_pred = (
        grad_pred
        + (total_cells * total_spots * valid_here * (1.0 / slide_rows - target / row_sums))[None, :]
    )
    shard_rows = lax.all_gather(grad_pred, "cell", axis=0, tiled=True)
    columns = genes_all
    grad_map = jnp.dot(columns, shard_rows, precision=highest)
    block_grad = lax.dot_general(mapping, shard_rows, (((1,), (1,)), ((), ())), precision=highest)
    grad_wide = block_grad
    grad_map, grad_wide = (grad_map, grad_wide)
    column_dot = lax.psum(jnp.sum(mapping * grad_map, axis=0), "cell")
    grad_logits = mapping * (grad_map - column_dot[None, :])
    grad_expr = lax.psum_scatter(grad_wide, "spot", scatter_dimension=1, tiled=True)
    first_spot = (lax.axis_index("spot") == 0).astype(jnp.float32)
    first_cell = (lax.axis_index("cell") == 0).astype(jnp.float32)
    totals = lax.psum(
        (
            first_spot * jnp.sum(cos_gene),
            first_cell * jnp.sum(valid_here * cos_spot),
            first_cell * jnp.sum(kl_terms),
            jnp.sum(mapping * mapping * weighted),
            jnp.sum(weighted * predicted * predicted),
            jnp.sum(weighted * smoothed * smoothed),
        ),
        ("spot", "cell"),
    )
    gene_loss = 1.0 - totals[0] / GENES
    spot_loss = 1.0 - totals[1] / nvalid
    density_loss = totals[2]
    rms_weights = total_cells * jnp.sqrt(totals[3] / (total_cells * nvalid))
    rms_pred = jnp.sqrt(totals[4] / (GENES * nvalid))
    rms_smooth = jnp.sqrt(totals[5] / (GENES * nvalid))
    return (
        gene_loss,
        spot_loss,
        density_loss,
        grad_logits,
        grad_expr,
        rms_weights,
        rms_pred,
        rms_smooth,
    )


def solution(mesh):
    placed = (
        P("cell", "spot"),
        P("cell", "spot"),
        P("cell", "spot"),
        P("spot"),
        P(),
        P(),
        P("spot", None),
    )
    return jax.shard_map(
        shards,
        mesh=mesh,
        in_specs=placed,
        out_specs=(P(), P(), P(), P("cell", "spot"), P("cell", "spot"), P(), P(), P()),
        check_vma=False,
    )
```

profile of v0, /device:TPU:0, one launch (start us, length us, event | category | flops | bytes accessed | tf_op | source)
XLA Modules:
  0.0 603.6 jit_solution(575941561613599674)
XLA Ops:
  8.0 1.7 reduce_max.9
  9.7 23.2 %pmax.7 = f32[1024]{0:T(1024)S(1)} all-reduce(f32[1024]{0:T(1024)S(1)} %reduce_max.9), channel_id=1, replica_groups=mesh['spot'=4,'cell'=8] {'cell'}, use_global_device_ids=true, to_apply=%region_1.0 | all-reduce | flops 1024 | bytes 8192 | tf_op jit(solution)/shard_map/pmax | solution.py:53
  33.2 17.1 %psum.119 = f32[1024]{0:T(1024)S(1)} all-reduce(f32[1024]{0:T(1024)S(1)} %fusion.3), channel_id=1, replica_groups=mesh['spot'=4,'cell'=8] {'cell'}, use_global_device_ids=true, to_apply=%region_3.4 | all-reduce | flops 1024 | bytes 8192 | tf_op jit(solution)/shard_map/psum | solution.py:55
  50.4 17.3 %convolution_bitcast_fusion = f32[2048,1024]{0,1:T(8,128)} fusion(f32[512,2048]{1,0:T(8,128)} %all-gather.3.cloned.1.call-done, f32[512,1024]{1,0:T(8,128)S(1)} %copy-done.3, f32[1024]{0:T(1024)S(1)} %psum.119, f32[1024]{0:T(1024)S(1)} %pmax.7), kind=kOutput, calls=%fused_computation.14 | convolution fusion | flops 12885950464 | bytes 14688256 | tf_op jit(solution)/shard_map/dot_general | solution.py:60
  72.3 60.4 %gather_fusion = s32[6144]{0:T(1024)} fusion(s32[4096]{0:T(1024)S(1)} %copy-done, s32[6144]{0:T(1024)S(1)} %broadcast_clamp_fusion), kind=kCustom, calls=%fused_computation.6 | custom fusion | bytes 73728 | tf_op jit(solution)/shard_map/gather | solution.py:45
  132.7 28.4 %gather_fusion.1 = s32[6144]{0:T(1024)S(1)} fusion(s32[4096]{0:T(1024)} %param.17, s32[6144]{0:T(1024)S(1)} %broadcast_clamp_fusion), kind=kCustom, calls=%fused_computation.7 | custom fusion | bytes 73728 | tf_op jit(solution)/shard_map/gather | solution.py:45
  167.2 2.4 fusion.40
  169.7 44.7 %reduce-scatter.3.cloned.1.call-done = f32[256,1024]{0,1:T(8,128)} async-done(((f32[2048,1024]{0,1:T(8,128)}), f32[256,1024]{0,1:T(8,128)}) %reduce-scatter.3.cloned.1.call-update) | async-done | bytes 1048592 | tf_op jit(solution)/shard_map/reduce_scatter | solution.py:59
  218.8 2.7 collective-permute-done.1
  221.5 3.2 concatenate.7
  224.7 4.7 gather_fusion.7
  229.4 4.7 gather_fusion.6
  234.1 4.7 gather_fusion.5
  238.7 4.7 gather_fusion.4
  243.4 4.7 gather_fusion.3
  248.1 4.7 gather_fusion.2
  252.7 7.7 %multiply_reduce_fusion.3 = (f32[1024]{0:T(1024)S(1)}, f32[256]{0:T(256)S(1)}, f32[]{:T(128)}, f32[256]{0:T(256)S(1)}, f32[256]{0:T(256)S(1)}, /*index=5*/f32[10...) fusion(f32[256,1024]{0,1:T(8,128)S(1)} %copy-done.6, f32[1024]{0:T(1024)S(1)} %get-tuple-element.85, ...), kind=kLoop, calls=%fused_computation.71 | loop fusion | flops 9433342 | bytes 9491464 | tf_op jit(solution)/shard_map/reduce_sum | solution.py:72
  260.4 35.2 %all-reduce.1 = (f32[1024]{0:T(1024)S(1)}, f32[1024]{0:T(1024)S(1)}, f32[1024]{0:T(1024)S(1)}, f32[1024]{0:T(1024)S(1)}) all-reduce(f32[1024]{0:T(1024)S(1)} %get-tuple-element.61, f32[1024]{0:T(1024)S(1)} %get-tuple-element.35, f32[1024]{0:T(1024)S(1)} %multiply_reduce_fusion.1, ...), channel_id=1, replica_groups=mesh['spot'=4,'cell'=8] {'cell'}, use_global_device_ids=true, to_apply=%region_27.29 | all-reduce | flops 4096 | bytes 32768 | tf_op jit(solution)/shard_map/psum | solution.py:70
  295.8 6.6 %all-reduce.2 = (f32[256]{0:T(256)S(1)}, f32[256]{0:T(256)S(1)}, f32[256]{0:T(256)S(1)}, f32[3]{0:T(128)S(1)}, f32[3]{0:T(128)S(1)}) all-reduce(f32[256]{0:T(256)S(1)} %get-tuple-element.36, f32[256]{0:T(256)S(1)} %get-tuple-element.38, f32[256]{0:T(256)S(1)} %get-tuple-element.39, ...), channel_id=1, replica_groups=mesh['spot'=4,'cell'=8] {'spot'}, use_global_device_ids=true, to_apply=%region_7.9 | all-reduce | flops 774 | bytes 6192 | tf_op jit(solution)/shard_map/psum | solution.py:80
  304.6 6.8 %scatter_custom_fusion = f32[256,1154]{0,1:T(8,128)S(1)} fusion(s32[1024]{0:T(1024)S(1)} %get-tuple-element.44, f32[256,1024]{0,1:T(8,128)S(1)} %subtract_divide_fusion, f32[]{:T(128)} %constant.106.clone.1, f32[1024]{0:T(1024)S(1)} %get-tuple-element.55), kind=kCustom, calls=%fused_computation.47 | custom fusion | flops 524288 | bytes 2234372 | tf_op jit(solution)/shard_map/scatter-add | solution.py:116
  311.5 7.0 %scatter_custom_fusion.1 = f32[256,1154]{0,1:T(8,128)S(1)} fusion(f32[256,1154]{0,1:T(8,128)S(1)} %scatter_custom_fusion, s32[1024]{0:T(1024)S(1)} %get-tuple-element.45, f32[256,1024]{0,1:T(8,128)S(1)} %subtract_divide_fusion, f32[1024]{0:T(1024)S(1)} %get-tuple-element.60), kind=kCustom, calls=%fused_computation.45 | custom fusion | flops 524288 | bytes 2234368 | tf_op jit(solution)/shard_map/scatter-add | solution.py:116
  318.5 7.1 %scatter_custom_fusion.2 = f32[256,1154]{0,1:T(8,128)S(1)} fusion(f32[256,1154]{0,1:T(8,128)S(1)} %scatter_custom_fusion.1, s32[1024]{0:T(1024)S(1)} %get-tuple-element.46, f32[256,1024]{0,1:T(8,128)S(1)} %subtract_divide_fusion, f32[1024]{0:T(1024)S(1)} %get-tuple-element.59), kind=kCustom, calls=%fused_computation.43 | custom fusion | flops 524288 | bytes 2234368 | tf_op jit(solution)/shard_map/scatter-add | solution.py:116
  325.5 7.1 %scatter_custom_fusion.3 = f32[256,1154]{0,1:T(8,128)S(1)} fusion(f32[256,1154]{0,1:T(8,128)S(1)} %scatter_custom_fusion.2, s32[1024]{0:T(1024)S(1)} %get-tuple-element.47, f32[256,1024]{0,1:T(8,128)S(1)} %subtract_divide_fusion, f32[1024]{0:T(1024)S(1)} %get-tuple-element.58), kind=kCustom, calls=%fused_computation.41 | custom fusion | flops 524288 | bytes 2234368 | tf_op jit(solution)/shard_map/scatter-add | solution.py:116
  332.6 7.4 %scatter_custom_fusion.4 = f32[256,1154]{0,1:T(8,128)S(1)} fusion(f32[256,1154]{0,1:T(8,128)S(1)} %scatter_custom_fusion.3, s32[1024]{0:T(1024)S(1)} %get-tuple-element.48, f32[256,1024]{0,1:T(8,128)S(1)} %subtract_divide_fusion, f32[1024]{0:T(1024)S(1)} %get-tuple-element.57), kind=kCustom, calls=%fused_computation.39 | custom fusion | flops 524288 | bytes 2234368 | tf_op jit(solution)/shard_map/scatter-add | solution.py:116
  340.0 7.0 %scatter_custom_fusion.5 = f32[256,1154]{0,1:T(8,128)S(1)} fusion(f32[256,1154]{0,1:T(8,128)S(1)} %scatter_custom_fusion.4, s32[1024]{0:T(1024)S(1)} %get-tuple-element.43, f32[256,1024]{0,1:T(8,128)S(1)} %subtract_divide_fusion, f32[1024]{0:T(1024)S(1)} %get-tuple-element.56), kind=kCustom, calls=%fused_computation.37 | custom fusion | flops 524288 | bytes 2234368 | tf_op jit(solution)/shard_map/scatter-add | solution.py:116
  350.7 3.2 collective-permute-start.3
  357.2 125.2 %all-gather.5.cloned.1.call-done = f32[2048,1024]{0,1:T(8,128)} async-done(((f32[256,1024]{0,1:T(8,128)}), f32[2048,1024]{0,1:T(8,128)}) %all-gather.5.cloned.1.call-update) | async-done | bytes 8388624 | tf_op jit(solution)/shard_map/all_gather | solution.py:126
  482.4 17.5 %fusion.53 = f32[512,2048]{1,0:T(8,128)} fusion(f32[2048,1024]{0,1:T(8,128)} %all-gather.5.cloned.1.call-done, f32[512,1024]{1,0:T(8,128)S(1)} %copy-done.4, f32[1024]{0:T(1024)S(1)} %copy-done.17, f32[1024]{0:T(1024)S(1)} %copy-done.14), kind=kOutput, calls=%fused_computation.144 | convolution fusion | flops 12885950464 | bytes 14688256 | tf_op jit(solution)/shard_map/dot_general | solution.py:129
  503.2 19.9 %multiply_reduce_fusion = (f32[]{:T(128)}, f32[1024]{0:T(1024)S(1)}, f32[1024,512]{0,1:T(8,128)}) fusion(f32[1024]{0:T(1024)S(1)} %get-tuple-element.85, f32[1024]{0:T(1024)S(1)} %copy-done.17, f32[512,1024]{1,0:T(8,128)S(1)} %copy-done.4, f32[1024]{0:T(1024)S(1)} %copy-done.14, f32[2048,1024]{0,1:T(8,128)} %all-gather.5.cloned.1.call-done, ...), kind=kOutput, calls=%fused_computation.19 | convolution fusion | flops 12888570880 | bytes 16793604 | tf_op jit(solution)/shard_map/dot_general | solution.py:128
  523.0 39.3 %all-reduce = (f32[]{:T(128)}, f32[]{:T(128)}, f32[]{:T(128)}, f32[]{:T(128)}, f32[]{:T(128)}, /*index=5*/f32[]{:T(128)}) all-reduce(f32[]{:T(128)S(6)} %mul.342, f32[]{:T(128)S(6)} %mul.349, f32[]{:T(128)S(6)} %mul.362, f32[]{:T(128)} %get-tuple-element.33, ...), channel_id=1, replica_groups=mesh['spot'=4,'cell'=8] {'spot','cell'}, use_global_device_ids=true, to_apply=%region_13.15 | all-reduce | flops 6 | bytes 48 | tf_op jit(solution)/shard_map/psum | solution.py:137
  566.4 21.4 %psum.132 = f32[1024]{0:T(1024)S(1)} all-reduce(f32[1024]{0:T(1024)S(1)} %get-tuple-element.34), channel_id=1, replica_groups=mesh['spot'=4,'cell'=8] {'cell'}, use_global_device_ids=true, to_apply=%region_41.43 | all-reduce | flops 1024 | bytes 8192 | tf_op jit(solution)/shard_map/psum | solution.py:132
  587.8 3.4 fusion.1
  (92 shorter events, 24.9 us)
Async XLA Ops:
  7.2 25.7 %copy-start.3 = (f32[512,1024]{1,0:T(8,128)S(1)}, f32[512,1024]{1,0:T(8,128)}, u32[]{:S(2)}) copy-start(f32[512,1024]{1,0:T(8,128)} %param.13) | copy-start | bytes 6291460
  7.2 43.2 %all-gather.3.cloned.1.call-start = ((), (), s32[]{:S(2)}) async-start(), calls=%async_computation.2 | async-start | bytes 5242880 | tf_op jit(solution)/shard_map/all_gather | solution.py:57
  7.9 206.5 %reduce-scatter.3.cloned.1.call-start = ((), (), s32[]{:S(2)}) async-start(), calls=%async_computation.3 | async-start | bytes 9437184 | tf_op jit(solution)/shard_map/reduce_scatter | solution.py:59
  32.9 34.8 %copy-start.13 = (f32[1024]{0:T(1024)}, f32[1024]{0:T(1024)S(1)}, u32[]{:S(2)}) copy-start(f32[1024]{0:T(1024)S(1)} %pmax.7) | copy-start | bytes 12292
  50.3 17.3 %copy-start.16 = (f32[1024]{0:T(1024)}, f32[1024]{0:T(1024)S(1)}, u32[]{:S(2)}) copy-start(f32[1024]{0:T(1024)S(1)} %psum.119) | copy-start | bytes 12292
  67.6 1.2 copy-start.9
  67.7 2.5 copy-start
  67.7 3.1 copy-start.11
  67.7 414.7 %all-gather.5.cloned.1.call-start = ((), (), s32[]{:S(2)}) async-start(), calls=%async_computation.4 | async-start | bytes 9437184 | tf_op jit(solution)/shard_map/all_gather | solution.py:126
  132.7 29.6 %copy-start.12 = (s32[1024,6]{0,1:T(8,128)S(1)}, s32[1024,6]{0,1:T(8,128)}, u32[]{:S(2)}) copy-start(s32[1024,6]{0,1:T(8,128)} %param.19) | copy-start | bytes 73732
  132.7 29.9 %copy-start.5 = (s32[6144]{0:T(1024)S(1)}, s32[6144]{0:T(1024)}, u32[]{:S(2)}) copy-start(s32[6144]{0:T(1024)} %gather_fusion) | copy-start | bytes 73732
  132.7 30.5 %copy-start.1 = (s32[4096]{0:T(1024)S(1)}, s32[4096]{0:T(1024)}, u32[]{:S(2)}) copy-start(s32[4096]{0:T(1024)} %param.18) | copy-start | bytes 49156
  132.7 32.4 %copy-start.10 = (f32[256,1024]{1,0:T(8,128)S(1)}, f32[256,1024]{1,0:T(8,128)}, u32[]{:S(2)}) copy-start(f32[256,1024]{1,0:T(8,128)} %param.15) | copy-start | bytes 3145732
  165.2 2.0 copy-start.2
  215.3 3.5 collective-permute-start
  216.8 4.7 collective-permute-start.1
  248.1 4.7 copy-start.6
  248.1 4.7 copy-start.7
  252.7 42.9 %copy-start.15 = (f32[1024]{0:T(1024)S(1)}, f32[1024]{0:T(1024)}, u32[]{:S(2)}) copy-start(f32[1024]{0:T(1024)} %param.16) | copy-start | bytes 12292
  347.0 1.0 copy-start.8
  348.0 5.9 collective-permute-start.2
  350.6 131.8 %copy-start.4 = (f32[512,1024]{1,0:T(8,128)S(1)}, f32[512,1024]{1,0:T(8,128)}, u32[]{:S(2)}) copy-start(f32[512,1024]{1,0:T(8,128)} %param.13) | copy-start | bytes 6291460
  350.7 131.8 %copy-start.14 = (f32[1024]{0:T(1024)S(1)}, f32[1024]{0:T(1024)}, u32[]{:S(2)}) copy-start(f32[1024]{0:T(1024)} %copy-done.13) | copy-start | bytes 12292
  350.7 131.8 %copy-start.17 = (f32[1024]{0:T(1024)S(1)}, f32[1024]{0:T(1024)}, u32[]{:S(2)}) copy-start(f32[1024]{0:T(1024)} %copy-done.16) | copy-start | bytes 12292
  350.7 4.1 collective-permute-start.3
  357.2 234.1 %reduce-scatter.5.cloned.1.call-start = ((), (), s32[]{:S(2)}) async-start(), calls=%async_computation.5 | async-start | bytes 5242880 | tf_op jit(solution)/shard_map/reduce_scatter | solution.py:134
Sparse Core Ops, SparseCore 0:
  9.5 37.1 all-gather.2
  67.8 146.5 reduce-scatter.2
  357.3 125.0 all-gather.4
  500.0 43.2 reduce-scatter.4
where the time goes:
time: 610 us; the launch traced here: 604 us
  waiting for transfers between devices  174 us (29%)
  blocking collectives  143 us (23%)
  local copies, waits for them, and re-layouts  129 us (21%)
  other arithmetic  67.4 us (11%)
  matrix products  54.6 us (9%)
  between operations  28 us (5%)
  starting transfers between devices  7.54 us (1%)
    all_gather x1, waiting for transfers between devices, shards(): shard_rows = lax.all_gather(grad_pred, 'cell', axis=0, tiled=True)  125 us
    gather x1, local copies, waits for them, and re-layouts, shards(): spot_valid[clamped] == 1  60.4 us
    reduce_scatter x1, waiting for transfers between devices, shards(): lax.psum_scatter(lax.dot_general(columns, mapping, (((0,), (0,)), ((), ()...  44.7 us
    scatter-add x6, other arithmetic, shards(): spread = spread.at[:, position[:, k]].add(linked[:, k][None, :] * spread_in)  42.3 us
    psum x1, blocking collectives, shards(): lax.psum((first_spot * jnp.sum(cos_gene), first_cell * jnp.sum(valid_here...  39.3 us
    psum x1, blocking collectives, shards(): lax.psum((jnp.sum(smoothed * spatial, axis=0), jnp.sum(smoothed * smoothe...  35.2 us
    gather x2, local copies, waits for them, and re-layouts, shards(): slide_ids[clamped] == slide_here[:, None]  28.9 us
    gather x6, local copies, waits for them, and re-layouts, shards(): jnp.take(padded, position[:, k], axis=1)  28 us
  transfers between devices with their start and end apart: 8, of which 4 were waited for; matrix products, arithmetic and copies ran while one was open for 21% of the time, Pallas kernels for 0%

commit v1 on v0

--- a/solution.py
+++ b/solution.py
@@ -123,7 +123,14 @@
         grad_pred
         + (total_cells * total_spots * valid_here * (1.0 / slide_rows - target / row_sums))[None, :]
     )
-    shard_rows = lax.all_gather(grad_pred, "cell", axis=0, tiled=True)
+    ways, here = (lax.axis_size("cell"), lax.axis_index("cell"))
+    shard_rows, reach = (grad_pred, 1)
+    while reach < ways:
+        theirs = lax.ppermute(shard_rows, "cell", [(d, d ^ reach) for d in range(ways)])
+        mine_first = jnp.concatenate([shard_rows, theirs], axis=0)
+        theirs_first = jnp.concatenate([theirs, shard_rows], axis=0)
+        shard_rows = jnp.where(here & reach == 0, mine_first, theirs_first)
+        reach = 2 * reach
     columns = genes_all
     grad_map = jnp.dot(columns, shard_rows, precision=highest)
     block_grad = lax.dot_general(mapping, shard_rows, (((1,), (1,)), ((), ())), precision=highest)

time: 610 us -> 749 us (1.23)
  waiting for transfers between devices: 174 us -> 305 us
    ppermute x0 -> x3, waiting for transfers between devices: none -> 256 us  [shards(): lax.ppermute(shard_rows, 'cell', [(d, d ^ reach) for d in range(ways)])]
    all_gather x1 -> x0, waiting for transfers between devices: 125 us -> none  [shards(): shard_rows = lax.all_gather(grad_pred, 'cell', axis=0, tiled=True)]
    select_n x0 -> x2, other arithmetic: none -> 8.23 us  [shards(): shard_rows = jnp.where(here & reach == 0, mine_first, theirs_first)]
  transfers between devices with their start and end apart: 8 -> 10, of which waited for: 4 -> 6; matrix products, arithmetic and copies ran while one was open for 21% -> 17% of each run, Pallas kernels for 0% -> 0%
where the time goes in v1:
time: 749 us; the launch traced here: 742 us
  waiting for transfers between devices  305 us (41%)
  blocking collectives  141 us (19%)
  local copies, waits for them, and re-layouts  129 us (17%)
  other arithmetic  73.6 us (10%)
  matrix products  58.6 us (8%)
  between operations  28 us (4%)
    ppermute x3, waiting for transfers between devices, shards(): lax.ppermute(shard_rows, 'cell', [(d, d ^ reach) for d in range(ways)])  256 us
    gather x1, local copies, waits for them, and re-layouts, shards(): spot_valid[clamped] == 1  60.4 us
    reduce_scatter x1, waiting for transfers between devices, shards(): lax.psum_scatter(lax.dot_general(columns, mapping, (((0,), (0,)), ((), ()...  44.6 us
    scatter-add x6, other arithmetic, shards(): spread = spread.at[:, position[:, k]].add(linked[:, k][None, :] * spread_in)  42.3 us
    psum x1, blocking collectives, shards(): lax.psum((first_spot * jnp.sum(cos_gene), first_cell * jnp.sum(valid_here...  37.7 us
    psum x1, blocking collectives, shards(): lax.psum((jnp.sum(smoothed * spatial, axis=0), jnp.sum(smoothed * smoothe...  35.2 us
    gather x2, local copies, waits for them, and re-layouts, shards(): slide_ids[clamped] == slide_here[:, None]  28.9 us
    gather x6, local copies, waits for them, and re-layouts, shards(): jnp.take(padded, position[:, k], axis=1)  28.1 us
  transfers between devices with their start and end apart: 10, of which 6 were waited for; matrix products, arithmetic and copies ran while one was open for 17% of the time, Pallas kernels for 0%

profile of v1, /device:TPU:0, one launch (start us, length us, event | category | flops | bytes accessed | tf_op | source)
XLA Modules:
  0.0 742.3 jit_solution(2370716538496674863)
XLA Ops:
  9.7 23.2 %pmax.7 = f32[1024]{0:T(1024)S(1)} all-reduce(f32[1024]{0:T(1024)S(1)} %reduce_max.9), channel_id=1, replica_groups=mesh['spot'=4,'cell'=8] {'cell'}, use_global_device_ids=true, to_apply=%region_1.0 | all-reduce | flops 1024 | bytes 8192 | tf_op jit(solution)/shard_map/pmax | solution.py:53
  33.2 17.1 %psum.119 = f32[1024]{0:T(1024)S(1)} all-reduce(f32[1024]{0:T(1024)S(1)} %fusion.7), channel_id=1, replica_groups=mesh['spot'=4,'cell'=8] {'cell'}, use_global_device_ids=true, to_apply=%region_3.4 | all-reduce | flops 1024 | bytes 8192 | tf_op jit(solution)/shard_map/psum | solution.py:55
  50.4 17.4 %convolution_bitcast_fusion = f32[2048,1024]{0,1:T(8,128)} fusion(f32[512,2048]{1,0:T(8,128)} %all-gather.2.cloned.1.call-done, f32[512,1024]{1,0:T(8,128)S(1)} %copy-done.3, f32[1024]{0:T(1024)S(1)} %psum.119, f32[1024]{0:T(1024)S(1)} %pmax.7), kind=kOutput, calls=%fused_computation.17 | convolution fusion | flops 12885950464 | bytes 14688256 | tf_op jit(solution)/shard_map/dot_general | solution.py:60
  72.4 60.4 %gather_fusion = s32[6144]{0:T(1024)} fusion(s32[4096]{0:T(1024)S(1)} %copy-done, s32[6144]{0:T(1024)S(1)} %broadcast_clamp_fusion), kind=kCustom, calls=%fused_computation.6 | custom fusion | bytes 73728 | tf_op jit(solution)/shard_map/gather | solution.py:45
  132.8 28.4 %gather_fusion.1 = s32[6144]{0:T(1024)S(1)} fusion(s32[4096]{0:T(1024)} %param.17, s32[6144]{0:T(1024)S(1)} %broadcast_clamp_fusion), kind=kCustom, calls=%fused_computation.7 | custom fusion | bytes 73728 | tf_op jit(solution)/shard_map/gather | solution.py:45
  169.9 44.6 %reduce-scatter.3.cloned.1.call-done = f32[256,1024]{0,1:T(8,128)} async-done(((f32[2048,1024]{0,1:T(8,128)}), f32[256,1024]{0,1:T(8,128)}) %reduce-scatter.3.cloned.1.call-update) | async-done | bytes 1048592 | tf_op jit(solution)/shard_map/reduce_scatter | solution.py:59
  221.6 3.2 concatenate.25
  224.8 4.7 gather_fusion.7
  229.5 4.7 gather_fusion.6
  234.2 4.7 gather_fusion.5
  238.9 4.7 gather_fusion.4
  243.6 4.7 gather_fusion.3
  248.3 4.7 gather_fusion.2
  253.0 7.7 %multiply_reduce_fusion.3 = (f32[1024]{0:T(1024)S(1)}, f32[256]{0:T(256)S(1)}, f32[]{:T(128)}, f32[256]{0:T(256)S(1)}, f32[256]{0:T(256)S(1)}, /*index=5*/f32[10...) fusion(f32[256,1024]{0,1:T(8,128)S(1)} %copy-done.6, f32[1024]{0:T(1024)S(1)} %get-tuple-element.85, ...), kind=kLoop, calls=%fused_computation.78 | loop fusion | flops 9433342 | bytes 9491464 | tf_op jit(solution)/shard_map/reduce_sum | solution.py:72
  260.6 35.2 %all-reduce.1 = (f32[1024]{0:T(1024)S(1)}, f32[1024]{0:T(1024)S(1)}, f32[1024]{0:T(1024)S(1)}, f32[1024]{0:T(1024)S(1)}) all-reduce(f32[1024]{0:T(1024)S(1)} %get-tuple-element.61, f32[1024]{0:T(1024)S(1)} %get-tuple-element.35, f32[1024]{0:T(1024)S(1)} %multiply_reduce_fusion.1, ...), channel_id=1, replica_groups=mesh['spot'=4,'cell'=8] {'cell'}, use_global_device_ids=true, to_apply=%region_27.29 | all-reduce | flops 4096 | bytes 32768 | tf_op jit(solution)/shard_map/psum | solution.py:70
  296.0 6.6 all-reduce.2
  304.9 6.8 scatter_custom_fusion
  311.7 7.0 scatter_custom_fusion.1
  318.7 7.1 scatter_custom_fusion.2
  325.8 7.1 scatter_custom_fusion.3
  332.8 7.4 scatter_custom_fusion.4
  340.2 7.0 scatter_custom_fusion.5
  348.7 3.0 collective-permute-start.3
  354.2 24.8 %collective-permute-done.4 = f32[256,1024]{0,1:T(8,128)S(1)} collective-permute-done((f32[256,1024]{0,1:T(8,128)S(1)}, f32[256,1024]{0,1:T(8,128)S(1)}, u32[]{:S(2)}, u32[]{:S(2)}) %collective-permute-start.4) | collective-permute-done | bytes 1048608 | tf_op jit(solution)/shard_map/ppermute | solution.py:129
  380.7 48.8 %collective-permute-done.5 = f32[512,1024]{0,1:T(8,128)} collective-permute-done((f32[512,1024]{0,1:T(8,128)}, f32[512,1024]{0,1:T(8,128)}, u32[]{:S(2)}, u32[]{:S(2)}) %collective-permute-start.5) | collective-permute-done | bytes 2097184 | tf_op jit(solution)/shard_map/ppermute | solution.py:129
  429.5 6.6 maximum_select_fusion.3
  436.1 182.9 %collective-permute-done.6 = f32[1024,1024]{0,1:T(8,128)} collective-permute-done((f32[1024,1024]{0,1:T(8,128)}, f32[1024,1024]{0,1:T(8,128)}, u32[]{:S(2)}, u32[]{:S(2)}) %collective-permute-start.6) | collective-permute-done | bytes 4194336 | tf_op jit(solution)/shard_map/ppermute | solution.py:129
  618.9 19.6 %fusion = f32[512,2048]{1,0:T(8,128)} fusion(f32[1024,1024]{0,1:T(8,128)} %collective-permute-done.6, f32[1024,1024]{0,1:T(8,128)} %maximum_select_fusion.3, pred[]{:T(512)S(6)} %eq.51, f32[512,1024]{1,0:T(8,128)S(1)} %copy-done.4, f32[1024]{0:T(1024)S(1)} %copy-done.16, f32[1024]{0:T(1024)S(1)} %copy-done.13), kind=kOutput, calls=%fused_computation.15 | convolution fusion | flops 12892241920 | bytes 14688257 | tf_op jit(solution)/shard_map/dot_general | solution.py:136
  641.8 21.6 %multiply_reduce_fusion = (f32[]{:T(128)}, f32[1024]{0:T(1024)S(1)}, f32[1024,512]{0,1:T(8,128)}) fusion(f32[1024]{0:T(1024)S(1)} %get-tuple-element.85, f32[1024]{0:T(1024)S(1)} %copy-done.16, f32[512,1024]{1,0:T(8,128)S(1)} %copy-done.4, f32[1024]{0:T(1024)S(1)} %copy-done.13, f32[512,2048]{1,0:T(8,128)} %all-gather.2.cloned.1.call-done, ...), kind=kOutput, calls=%fused_computation.26 | convolution fusion | flops 12894862336 | bytes 16793604 | tf_op jit(solution)/shard_map/dot_general | solution.py:135
  663.4 37.7 %all-reduce = (f32[]{:T(128)}, f32[]{:T(128)}, f32[]{:T(128)}, f32[]{:T(128)}, f32[]{:T(128)}, /*index=5*/f32[]{:T(128)}) all-reduce(f32[]{:T(128)S(6)} %mul.342, f32[]{:T(128)S(6)} %mul.349, f32[]{:T(128)S(6)} %mul.362, f32[]{:T(128)} %get-tuple-element.33, ...), channel_id=1, replica_groups=mesh['spot'=4,'cell'=8] {'spot','cell'}, use_global_device_ids=true, to_apply=%region_13.15 | all-reduce | flops 6 | bytes 48 | tf_op jit(solution)/shard_map/psum | solution.py:144
  705.2 21.3 %psum.132 = f32[1024]{0:T(1024)S(1)} all-reduce(f32[1024]{0:T(1024)S(1)} %get-tuple-element.34), channel_id=1, replica_groups=mesh['spot'=4,'cell'=8] {'cell'}, use_global_device_ids=true, to_apply=%region_41.43 | all-reduce | flops 1024 | bytes 8192 | tf_op jit(solution)/shard_map/psum | solution.py:139
  726.5 3.4 fusion.5
  (95 shorter events, 30.4 us)
Async XLA Ops:
  7.2 25.7 %copy-start.3 = (f32[512,1024]{1,0:T(8,128)S(1)}, f32[512,1024]{1,0:T(8,128)}, u32[]{:S(2)}) copy-start(f32[512,1024]{1,0:T(8,128)} %param.13) | copy-start | bytes 6291460
  7.2 43.2 %all-gather.2.cloned.1.call-start = ((), (), s32[]{:S(2)}) async-start(), calls=%async_computation.2 | async-start | bytes 5242880 | tf_op jit(solution)/shard_map/all_gather | solution.py:57
  7.9 206.6 %reduce-scatter.3.cloned.1.call-start = ((), (), s32[]{:S(2)}) async-start(), calls=%async_computation.3 | async-start | bytes 9437184 | tf_op jit(solution)/shard_map/reduce_scatter | solution.py:59
  32.9 34.9 %copy-start.12 = (f32[1024]{0:T(1024)}, f32[1024]{0:T(1024)S(1)}, u32[]{:S(2)}) copy-start(f32[1024]{0:T(1024)S(1)} %pmax.7) | copy-start | bytes 12292
  50.3 17.4 %copy-start.15 = (f32[1024]{0:T(1024)}, f32[1024]{0:T(1024)S(1)}, u32[]{:S(2)}) copy-start(f32[1024]{0:T(1024)S(1)} %psum.119) | copy-start | bytes 12292
  67.7 1.2 copy-start.8
  67.8 2.5 copy-start
  67.8 3.1 copy-start.10
  67.8 662.1 %reduce-scatter.5.cloned.1.call-start = ((), (), s32[]{:S(2)}) async-start(), calls=%async_computation.4 | async-start | bytes 5242880 | tf_op jit(solution)/shard_map/reduce_scatter | solution.py:141
  132.8 29.6 %copy-start.11 = (s32[1024,6]{0,1:T(8,128)S(1)}, s32[1024,6]{0,1:T(8,128)}, u32[]{:S(2)}) copy-start(s32[1024,6]{0,1:T(8,128)} %param.19) | copy-start | bytes 73732
  132.8 29.9 %copy-start.5 = (s32[6144]{0:T(1024)S(1)}, s32[6144]{0:T(1024)}, u32[]{:S(2)}) copy-start(s32[6144]{0:T(1024)} %gather_fusion) | copy-start | bytes 73732
  132.8 30.5 %copy-start.1 = (s32[4096]{0:T(1024)S(1)}, s32[4096]{0:T(1024)}, u32[]{:S(2)}) copy-start(s32[4096]{0:T(1024)} %param.18) | copy-start | bytes 49156
  132.8 32.5 %copy-start.9 = (f32[256,1024]{1,0:T(8,128)S(1)}, f32[256,1024]{1,0:T(8,128)}, u32[]{:S(2)}) copy-start(f32[256,1024]{1,0:T(8,128)} %param.15) | copy-start | bytes 3145732
  165.4 2.0 copy-start.2
  215.4 3.5 collective-permute-start
  216.9 4.7 collective-permute-start.1
  248.3 4.7 copy-start.6
  248.3 4.7 copy-start.7
  253.0 42.9 %copy-start.14 = (f32[1024]{0:T(1024)S(1)}, f32[1024]{0:T(1024)}, u32[]{:S(2)}) copy-start(f32[1024]{0:T(1024)} %param.16) | copy-start | bytes 12292
  347.2 4.5 collective-permute-start.2
  348.7 3.9 collective-permute-start.3
  354.1 24.9 %collective-permute-start.4 = (f32[256,1024]{0,1:T(8,128)S(1)}, f32[256,1024]{0,1:T(8,128)S(1)}, u32[]{:S(2)}, u32[]{:S(2)}) collective-permute-start(f32[256,1024]{0,1:T(8,128)S(1)} %broadcast_add_fusion), channel_id=1, source_target_pairs={{0,1},{1,0},{2,3},{3,2},{4,5},{5,4},{6,7},{7,6},{8,9},{9,8},{10,11... | collective-permute-start | bytes 3145736 | tf_op jit(solution)/shard_map/ppermute | solution.py:129
  380.7 48.8 %collective-permute-start.5 = (f32[512,1024]{0,1:T(8,128)}, f32[512,1024]{0,1:T(8,128)}, u32[]{:S(2)}, u32[]{:S(2)}) collective-permute-start(f32[512,1024]{0,1:T(8,128)} %maximum_select_fusion.4), channel_id=1, source_target_pairs={{0,2},{1,3},{2,0},{3,1},{4,6},{5,7},{6,4},{7,5},{8,10},{9,11},{10,... | collective-permute-start | bytes 6291464 | tf_op jit(solution)/shard_map/ppermute | solution.py:129
  380.7 238.2 %copy-start.4 = (f32[512,1024]{1,0:T(8,128)S(1)}, f32[512,1024]{1,0:T(8,128)}, u32[]{:S(2)}) copy-start(f32[512,1024]{1,0:T(8,128)} %param.13) | copy-start | bytes 6291460
  380.7 238.2 %copy-start.13 = (f32[1024]{0:T(1024)S(1)}, f32[1024]{0:T(1024)}, u32[]{:S(2)}) copy-start(f32[1024]{0:T(1024)} %copy-done.12) | copy-start | bytes 12292
  380.7 238.2 %copy-start.16 = (f32[1024]{0:T(1024)S(1)}, f32[1024]{0:T(1024)}, u32[]{:S(2)}) copy-start(f32[1024]{0:T(1024)} %copy-done.15) | copy-start | bytes 12292
  436.0 182.9 %collective-permute-start.6 = (f32[1024,1024]{0,1:T(8,128)}, f32[1024,1024]{0,1:T(8,128)}, u32[]{:S(2)}, u32[]{:S(2)}) collective-permute-start(f32[1024,1024]{0,1:T(8,128)} %maximum_select_fusion.3), channel_id=1, source_target_pairs={{0,4},{1,5},{2,6},{3,7},{4,0},{5,1},{6,2},{7,3},{8,12},{9,13},{10,... | collective-permute-start | bytes 12582920 | tf_op jit(solution)/shard_map/ppermute | solution.py:129
Sparse Core Ops, SparseCore 0:
  9.5 37.1 all-gather.1
  67.9 146.5 reduce-scatter.2
  638.7 41.4 reduce-scatter.4
